TPU v7x, 128 devices: a whole 4x4x4 slice. The times are simulated.
128 devices in a mesh: row: 8 (over y_lo, x), col: 16 (over y_hi, z, core).
Axes of the slice: x: 4, y: 4 (y_hi: 2, y_lo: 2; y = y_hi * 2 + y_lo), z: 4, core: 2. Of those that a mesh axis runs over, the one named last changes fastest.
Arguments:
- factor_panel: bfloat16 [12288, 98304], P('row', 'col'), may hold values from -1 to 1, as said below
- normals: bfloat16 [98304, 128], P(('col', 'row')), may hold values from -6 to 6
- bond_vectors: float32 [3, 4096, 12], P(None, ('col', 'row')), may hold values from -9 to 9
- neighbours: int32 [4096, 12], P(('col', 'row')), may hold values from 0 to 175
- send_atoms: int32 [128, 16], P(('col', 'row')), may hold values from 0 to 31
- radial_weight: bfloat16 [128, 128], replicated, may hold values from -1.5 to 1.5
- radial_bias: float32 [128], replicated, may hold values from -3 to 3
- middle_weight: bfloat16 [128, 128], replicated, may hold values from -0.5 to 0.5
- middle_bias: float32 [128], replicated, may hold values from -3 to 3
- output_weight: float32 [128], replicated, may hold values from -0.5 to 0.5
Outputs:
- atom_energy: float32 [4096, 128], P(('col', 'row'))
- forces: float32 [3, 4096, 128], P(None, ('col', 'row'))
Inputs may be any that keep to these rules, and one draw needn't show every extreme that they name: `factor_panel`: entries above the factor's diagonal are zero.
All inputs are finite; a program needn't handle non-finite values.
Results may differ from a plain program's by a relative error of at most 0.0052.
Values may be sent and summed in bfloat16 or wider, within the bound.
A program may use at most 128 MiB of HBM per device.

v0:
```python
import jax
import jax.numpy as jnp
from jax import lax
from jax.sharding import PartitionSpec as P

TILE = 16


def with_halo(cells, sides, width):
    for axis, dim in sides:
        count = lax.axis_size(axis)
        head = lax.slice_in_dim(cells, 0, width, axis=dim)
        tail = lax.slice_in_dim(cells, cells.shape[dim] - width, cells.shape[dim], axis=dim)
        cells = jnp.concatenate(
            [
                lax.ppermute(tail, axis, [(i, (i + 1) % count) for i in range(count)]),
                cells,
                lax.ppermute(head, axis, [((i + 1) % count, i) for i in range(count)]),
            ],
            axis=dim,
        )
    return cells


def pair_terms(
    own_disp,
    near_disp,
    bond_block,
    radial_weight,
    radial_bias,
    middle_weight,
    middle_bias,
    output_weight,
):
    vectors = bond_block[:, :, :, None] + near_disp - own_disp[:, :, None, :]
    squared = jnp.sum(vectors * vectors, axis=0)
    count = radial_weight.shape[0]
    centres = 30.0 * jnp.arange(count, dtype=jnp.float32) / (count - 1)
    spread = 90.0 / (count - 1)
    scaled = (squared[..., None] - centres) / spread
    basis = jnp.exp(-scaled * scaled)
    flat_basis = basis.reshape(-1, count)
    flat_scaled = scaled.reshape(-1, count)
    first = jnp.tanh(
        jnp.dot(flat_basis.astype(jnp.bfloat16), radial_weight, preferred_element_type=jnp.float32)
        + radial_bias
    )
    second = jnp.tanh(
        jnp.dot(first.astype(jnp.bfloat16), middle_weight, preferred_element_type=jnp.float32)
        + middle_bias
    )
    energies = jnp.sum(second * output_weight, axis=-1)
    back_second = ((1.0 - second * second) * output_weight).astype(jnp.bfloat16)
    back_first = (
        jnp.dot(back_second, middle_weight.T, preferred_element_type=jnp.float32)
        * (1.0 - first * first)
    ).astype(jnp.bfloat16)
    radial_grad = jnp.dot(back_first, radial_weight.T, preferred_element_type=jnp.float32)
    slopes = jnp.sum(radial_grad * flat_basis * (-2.0 / spread) * flat_scaled, axis=-1)
    shape = squared.shape
    atom_part = 0.5 * jnp.sum(energies.reshape(shape), axis=1)
    force_part = 2.0 * jnp.sum(slopes.reshape(shape)[None] * vectors, axis=2)
    return (atom_part, force_part)


def per_device(
    factor_panel,
    normals,
    bond_vectors,
    neighbours,
    send_atoms,
    radial_weight,
    radial_bias,
    middle_weight,
    middle_bias,
    output_weight,
):
    samples = normals.shape[1]
    local_rows = factor_panel.shape[0]
    partial_value = jnp.dot(
        factor_panel,
        lax.all_gather(normals, "row", axis=0, tiled=True),
        preferred_element_type=jnp.float32,
    )
    col_count = lax.axis_size("col")
    col_index = lax.axis_index("col")
    slab_rows = local_rows // col_count
    total = lax.psum(partial_value, "col")
    slab = lax.dynamic_slice_in_dim(total, col_index * slab_rows, slab_rows, 0)
    rows_count = lax.axis_size("row")
    row_index = lax.axis_index("row")
    tiles = slab_rows // TILE
    whole = lax.all_gather(slab, "row", axis=0, tiled=True)
    ordered = (
        whole.reshape(rows_count, tiles, TILE, samples)
        .transpose(1, 0, 2, 3)
        .reshape(rows_count * slab_rows, samples)
    )
    domain = lax.dynamic_slice_in_dim(ordered, row_index * slab_rows, slab_rows, 0)
    domain_atoms = bond_vectors.shape[1]
    neighbour_count = bond_vectors.shape[2]
    displacements = domain.reshape(3, domain_atoms, samples)
    sent = jnp.take(displacements, send_atoms[0], axis=1)
    beside_all = with_halo(sent[None, None], (("row", 0), ("col", 1)), 1)
    halo_atoms = jnp.moveaxis(beside_all, 2, 0).reshape(3, 9 * sent.shape[1], samples)
    pool = jnp.concatenate([displacements, halo_atoms], axis=1)
    nearby = jnp.take(pool, neighbours.reshape(-1), axis=1).reshape(
        3, domain_atoms, neighbour_count, samples
    )
    block_count = domain_atoms // 8
    own_blocks = displacements.reshape(3, block_count, 8, samples).transpose(1, 0, 2, 3)
    near_blocks = nearby.reshape(3, block_count, 8, neighbour_count, samples).transpose(
        1, 0, 2, 3, 4
    )
    bond_blocks = bond_vectors.reshape(3, block_count, 8, neighbour_count).transpose(1, 0, 2, 3)
    energy_blocks, force_blocks = lax.map(
        lambda items: pair_terms(
            items[0],
            items[1],
            items[2],
            radial_weight,
            radial_bias,
            middle_weight,
            middle_bias,
            output_weight,
        ),
        (own_blocks, near_blocks, bond_blocks),
    )
    atom_energy = energy_blocks.reshape(domain_atoms, samples)
    forces = force_blocks.transpose(1, 0, 2, 3).reshape(3, domain_atoms, samples)
    return (atom_energy, forces)


def solution(mesh):
    return jax.shard_map(
        per_device,
        mesh=mesh,
        in_specs=(
            P("row", "col"),
            P(("col", "row"), None),
            P(None, ("col", "row"), None),
            P(("col", "row"), None),
            P(("col", "row"), None),
            P(),
            P(),
            P(),
            P(),
            P(),
        ),
        out_specs=(P(("col", "row"), None), P(None, ("col", "row"), None)),
        check_vma=False,
    )
```

profile of v0, /device:TPU:103, one launch (start us, length us, event | category | flops | bytes accessed | tf_op | source)
XLA Modules:
  0.0 323.6 jit_solution(1270470169724800918)
XLA Ops:
  8.0 35.4 %all-gather.2.cloned.1.call-done = bf16[6144,128]{1,0:T(8,128)(2,1)} async-done(((bf16[768,128]{1,0:T(8,128)(2,1)}), bf16[6144,128]{1,0:T(8,128)(2,1)}) %all-gather.2.cloned.1.call-update) | async-done | bytes 1572880 | tf_op jit(solution)/shard_map/all_gather | solution.py:82
  43.4 10.2 %fusion.22 = f32[1536,128]{1,0:T(8,128)} fusion(bf16[1536,6144]{1,0:T(8,128)(2,1)} %param.12, bf16[6144,128]{1,0:T(8,128)(2,1)} %all-gather.2.cloned.1.call-done), kind=kOutput, calls=%fused_computation.54 | convolution fusion | flops 2415919104 | bytes 21233664 | tf_op jit(solution)/shard_map/dot_general | solution.py:80
  53.9 147.7 %all-reduce.2.cloned.1.call-done = f32[1536,128]{1,0:T(8,128)} async-done(((f32[1536,128]{1,0:T(8,128)}), f32[1536,128]{1,0:T(8,128)}) %all-reduce.2.cloned.1.call-update) | async-done | bytes 786448 | tf_op jit(solution)/shard_map/psum | solution.py:88
  202.4 22.9 %all_gather.7 = f32[768,128]{1,0:T(8,128)S(1)} all-gather(f32[96,128]{1,0:T(8,128)S(1)} %constant_dynamic-slice_fusion.1), channel_id=1, replica_groups=mesh['row'=8,'col'=16] {'row'}, dimensions={0}, use_global_device_ids=true | all-gather | bytes 442368 | tf_op jit(solution)/shard_map/all_gather | solution.py:93
  226.1 0.9 collective-permute-start
  227.8 1.2 collective-permute-done
  228.9 2.9 collective-permute-done.1
  231.9 9.4 %collective-permute-start.2 = (f32[3,1,3,16,128]{4,2,3,1,0:T(4,128)S(1)}, f32[3,1,3,16,128]{4,2,3,1,0:T(4,128)S(1)}, u32[]{:S(2)}, u32[]{:S(2)}) collective-permute-start(f32[3,1,3,16,128]{4,2,3,1,0:T(4,128)S(1)} %pad_maximum_fusion.2), channel_id=1, source_target_pairs={{0,1},{1,2},{2,3},{3,4},{4,5},{5,6},{6,7},{7,8},{8,9},{9,10},{10,1... | collective-permute-start | bytes 221192 | tf_op jit(solution)/shard_map/ppermute | solution.py:16
  241.3 1.6 collective-permute-done.2
  242.9 6.0 %collective-permute-done.3 = f32[3,1,3,16,128]{4,2,3,1,0:T(4,128)S(1)} collective-permute-done((f32[3,1,3,16,128]{4,2,3,1,0:T(4,128)S(1)}, f32[3,1,3,16,128]{4,2,3,1,0:T(4,128)S(1)}, u32[]{:S(2)}, u32[]{:S(2)}) %collective-permute-start.3) | collective-permute-done | bytes 73760 | tf_op jit(solution)/shard_map/ppermute | solution.py:18
  249.1 2.0 gather_fusion.1
  251.4 64.7 %while.14 = (s32[]{:T(128)}, f32[4,8,128]{2,1,0:T(8,128)S(1)}, f32[4,3,8,128]{3,2,1,0:T(8,128)S(1)}, f32[4,3,8,12]{3,2,0,1:T(8,128)S(1)}, f32[4,3,8,12,128]{4,3,...) while((s32[]{:T(128)}, f32[4,8,128]{2,1,0:T(8,128)S(1)}, ...), condition=%wide.region_7.8_spmd, body=%wide.region_1.7_spmd.sunk | while | flops 1651777664 | bytes 57794740 | solution.py:116
  251.6 2.5 fusion.42
  254.0 4.5 %multiply_reduce_fusion.7 = (f32[12288]{0:T(1024)S(1)}, f32[12288,128]{1,0:T(8,128)}) fusion(f32[128]{0:T(128)S(1)} %get-tuple-element.295, f32[128]{0:T(128)S(1)} %get-tuple-element.294, bf16[128,128]{1,0:T(8,128)(2,1)S(1)} %get-tuple-element.293, f32[12288,128]{1,0:T(8,128)S(1)} %fusion.42), kind=kOutput, calls=%fused_computation.15.clone.1 | convolution fusion | flops 408932352 | bytes 12665856 | tf_op jit(solution)/shard_map/while/body/eval_jaxpr/dot_general | solution.py:49
  258.6 8.7 %fusion.43 = f32[12288]{0:T(1024)S(1)} fusion(f32[128]{0:T(128)S(1)} %iota_multiply_fusion.2, f32[12288]{0:T(1024)S(1)} %sub.114, bf16[128,128]{1,0:T(8,128)(2,1)S(1)} %get-tuple-element.291, bf16[128,128]{1,0:T(8,128)(2,1)S(1)} %get-tuple-element.293, f32[12288,128]{1,0:T(8,128)} %copy-done, f32[12288,128]{1,0:T(8,128)} %get-tuple-element.258, ...), kind=kOutput, calls=%fused_computation.23.clone.1 | convolution fusion | flops 830459904 | bytes 12747776 | tf_op jit(solution)/shard_map/while/body/eval_jaxpr/dot_general | solution.py:58
  267.8 2.5 fusion.42
  270.2 4.5 %multiply_reduce_fusion.7 = (f32[12288]{0:T(1024)S(1)}, f32[12288,128]{1,0:T(8,128)}) fusion(f32[128]{0:T(128)S(1)} %get-tuple-element.295, f32[128]{0:T(128)S(1)} %get-tuple-element.294, bf16[128,128]{1,0:T(8,128)(2,1)S(1)} %get-tuple-element.293, f32[12288,128]{1,0:T(8,128)S(1)} %fusion.42), kind=kOutput, calls=%fused_computation.15.clone.1 | convolution fusion | flops 408932352 | bytes 12665856 | tf_op jit(solution)/shard_map/while/body/eval_jaxpr/dot_general | solution.py:49
  274.8 8.7 %fusion.43 = f32[12288]{0:T(1024)S(1)} fusion(f32[128]{0:T(128)S(1)} %iota_multiply_fusion.2, f32[12288]{0:T(1024)S(1)} %sub.114, bf16[128,128]{1,0:T(8,128)(2,1)S(1)} %get-tuple-element.291, bf16[128,128]{1,0:T(8,128)(2,1)S(1)} %get-tuple-element.293, f32[12288,128]{1,0:T(8,128)} %copy-done, f32[12288,128]{1,0:T(8,128)} %get-tuple-element.258, ...), kind=kOutput, calls=%fused_computation.23.clone.1 | convolution fusion | flops 830459904 | bytes 12747776 | tf_op jit(solution)/shard_map/while/body/eval_jaxpr/dot_general | solution.py:58
  283.9 2.5 fusion.42
  286.4 4.5 %multiply_reduce_fusion.7 = (f32[12288]{0:T(1024)S(1)}, f32[12288,128]{1,0:T(8,128)}) fusion(f32[128]{0:T(128)S(1)} %get-tuple-element.295, f32[128]{0:T(128)S(1)} %get-tuple-element.294, bf16[128,128]{1,0:T(8,128)(2,1)S(1)} %get-tuple-element.293, f32[12288,128]{1,0:T(8,128)S(1)} %fusion.42), kind=kOutput, calls=%fused_computation.15.clone.1 | convolution fusion | flops 408932352 | bytes 12665856 | tf_op jit(solution)/shard_map/while/body/eval_jaxpr/dot_general | solution.py:49
  290.9 8.7 %fusion.43 = f32[12288]{0:T(1024)S(1)} fusion(f32[128]{0:T(128)S(1)} %iota_multiply_fusion.2, f32[12288]{0:T(1024)S(1)} %sub.114, bf16[128,128]{1,0:T(8,128)(2,1)S(1)} %get-tuple-element.291, bf16[128,128]{1,0:T(8,128)(2,1)S(1)} %get-tuple-element.293, f32[12288,128]{1,0:T(8,128)} %copy-done, f32[12288,128]{1,0:T(8,128)} %get-tuple-element.258, ...), kind=kOutput, calls=%fused_computation.23.clone.1 | convolution fusion | flops 830459904 | bytes 12747776 | tf_op jit(solution)/shard_map/while/body/eval_jaxpr/dot_general | solution.py:58
  300.1 2.5 fusion.42
  302.6 4.5 %multiply_reduce_fusion.7 = (f32[12288]{0:T(1024)S(1)}, f32[12288,128]{1,0:T(8,128)}) fusion(f32[128]{0:T(128)S(1)} %get-tuple-element.295, f32[128]{0:T(128)S(1)} %get-tuple-element.294, bf16[128,128]{1,0:T(8,128)(2,1)S(1)} %get-tuple-element.293, f32[12288,128]{1,0:T(8,128)S(1)} %fusion.42), kind=kOutput, calls=%fused_computation.15.clone.1 | convolution fusion | flops 408932352 | bytes 12665856 | tf_op jit(solution)/shard_map/while/body/eval_jaxpr/dot_general | solution.py:49
  307.1 8.7 %fusion.43 = f32[12288]{0:T(1024)S(1)} fusion(f32[128]{0:T(128)S(1)} %iota_multiply_fusion.2, f32[12288]{0:T(1024)S(1)} %sub.114, bf16[128,128]{1,0:T(8,128)(2,1)S(1)} %get-tuple-element.291, bf16[128,128]{1,0:T(8,128)(2,1)S(1)} %get-tuple-element.293, f32[12288,128]{1,0:T(8,128)} %copy-done, f32[12288,128]{1,0:T(8,128)} %get-tuple-element.258, ...), kind=kOutput, calls=%fused_computation.23.clone.1 | convolution fusion | flops 830459904 | bytes 12747776 | tf_op jit(solution)/shard_map/while/body/eval_jaxpr/dot_general | solution.py:58
  (98 shorter events, 5.7 us)
Async XLA Ops:
  7.2 36.2 %all-gather.2.cloned.1.call-start = ((), (), s32[]{:S(2)}) async-start(), calls=%async_computation | async-start | bytes 1769472 | tf_op jit(solution)/shard_map/all_gather | solution.py:82
  7.9 45.7 %copy-start.5 = (s32[32,12]{0,1:T(8,128)S(1)}, s32[32,12]{0,1:T(8,128)}, u32[]{:S(2)}) copy-start(s32[32,12]{0,1:T(8,128)} %param.15) | copy-start | bytes 4612
  7.9 45.9 %copy-start.8 = (s32[1,16]{1,0:T(1,128)S(1)}, s32[1,16]{1,0:T(1,128)}, u32[]{:S(2)}) copy-start(s32[1,16]{1,0:T(1,128)} %param.16) | copy-start | bytes 196
  7.9 219.7 %copy-start.2 = (f32[3,32,12]{1,2,0:T(8,128)S(1)}, f32[3,32,12]{1,2,0:T(8,128)}, u32[]{:S(2)}) copy-start(f32[3,32,12]{1,2,0:T(8,128)} %param.14) | copy-start | bytes 13828
  7.9 193.6 %all-reduce.2.cloned.1.call-start = ((), (), s32[]{:S(2)}) async-start(), calls=%async_computation.1 | async-start | bytes 1572864 | tf_op jit(solution)/shard_map/psum | solution.py:88
  53.6 197.7 %copy-start.1 = (bf16[128,128]{1,0:T(8,128)(2,1)S(1)}, bf16[128,128]{1,0:T(8,128)(2,1)}, u32[]{:S(2)}) copy-start(bf16[128,128]{1,0:T(8,128)(2,1)} %param.19) | copy-start | bytes 98308
  53.6 197.8 %copy-start.3 = (f32[128]{0:T(128)S(1)}, f32[128]{0:T(128)}, u32[]{:S(2)}) copy-start(f32[128]{0:T(128)} %param.20) | copy-start | bytes 1540
  53.6 197.8 %copy-start.4 = (f32[128]{0:T(128)S(1)}, f32[128]{0:T(128)}, u32[]{:S(2)}) copy-start(f32[128]{0:T(128)} %param.21) | copy-start | bytes 1540
  53.6 197.8 %copy-start.6 = (bf16[128,128]{1,0:T(8,128)(2,1)S(1)}, bf16[128,128]{1,0:T(8,128)(2,1)}, u32[]{:S(2)}) copy-start(bf16[128,128]{1,0:T(8,128)(2,1)} %param.17) | copy-start | bytes 98308
  53.6 197.8 %copy-start.9 = (f32[128]{0:T(128)S(1)}, f32[128]{0:T(128)}, u32[]{:S(2)}) copy-start(f32[128]{0:T(128)} %param.18) | copy-start | bytes 1540
  226.1 2.8 collective-permute-start
  227.0 4.9 %collective-permute-start.1 = (f32[1,1,3,16,128]{4,2,3,1,0:T(4,128)S(1)}, f32[1,1,3,16,128]{4,2,3,1,0:T(4,128)S(1)}, u32[]{:S(2)}, u32[]{:S(2)}) collective-permute-start(f32[1,1,3,16,128]{4,2,3,1,0:T(4,128)S(1)} %bitcast_select_fusion), channel_id=1, source_target_pairs={{16,0},{32,16},{48,32},{64,48},{80,64},{96,80},{112,96},{0,112},{1... | collective-permute-start | bytes 73736 | tf_op jit(solution)/shard_map/ppermute | solution.py:18
  231.9 11.0 %collective-permute-start.2 = (f32[3,1,3,16,128]{4,2,3,1,0:T(4,128)S(1)}, f32[3,1,3,16,128]{4,2,3,1,0:T(4,128)S(1)}, u32[]{:S(2)}, u32[]{:S(2)}) collective-permute-start(f32[3,1,3,16,128]{4,2,3,1,0:T(4,128)S(1)} %pad_maximum_fusion.2), channel_id=1, source_target_pairs={{0,1},{1,2},{2,3},{3,4},{4,5},{5,6},{6,7},{7,8},{8,9},{9,10},{10,1... | collective-permute-start | bytes 221192 | tf_op jit(solution)/shard_map/ppermute | solution.py:16
  241.3 7.7 %collective-permute-start.3 = (f32[3,1,3,16,128]{4,2,3,1,0:T(4,128)S(1)}, f32[3,1,3,16,128]{4,2,3,1,0:T(4,128)S(1)}, u32[]{:S(2)}, u32[]{:S(2)}) collective-permute-start(f32[3,1,3,16,128]{4,2,3,1,0:T(4,128)S(1)} %pad_maximum_fusion.2), channel_id=1, source_target_pairs={{1,0},{2,1},{3,2},{4,3},{5,4},{6,5},{7,6},{8,7},{9,8},{10,9},{11,1... | collective-permute-start | bytes 221192 | tf_op jit(solution)/shard_map/ppermute | solution.py:18
  254.0 4.5 %copy-start = (f32[12288,128]{1,0:T(8,128)}, f32[12288,128]{1,0:T(8,128)S(1)}, u32[]{:S(2)}) copy-start(f32[12288,128]{1,0:T(8,128)S(1)} %fusion.42) | copy-start | bytes 18874372 | tf_op jit(solution)/shard_map/while
  270.2 4.5 %copy-start = (f32[12288,128]{1,0:T(8,128)}, f32[12288,128]{1,0:T(8,128)S(1)}, u32[]{:S(2)}) copy-start(f32[12288,128]{1,0:T(8,128)S(1)} %fusion.42) | copy-start | bytes 18874372 | tf_op jit(solution)/shard_map/while
  286.4 4.5 %copy-start = (f32[12288,128]{1,0:T(8,128)}, f32[12288,128]{1,0:T(8,128)S(1)}, u32[]{:S(2)}) copy-start(f32[12288,128]{1,0:T(8,128)S(1)} %fusion.42) | copy-start | bytes 18874372 | tf_op jit(solution)/shard_map/while
  302.6 4.5 %copy-start = (f32[12288,128]{1,0:T(8,128)}, f32[12288,128]{1,0:T(8,128)S(1)}, u32[]{:S(2)}) copy-start(f32[12288,128]{1,0:T(8,128)S(1)} %fusion.42) | copy-start | bytes 18874372 | tf_op jit(solution)/shard_map/while
  316.1 0.6 copy-start.7
Sparse Core Ops, SparseCore 0:
  9.6 33.7 all-gather.1
  53.8 147.7 all-reduce.1
where the time goes:
time: 324 us
  waiting for transfers between devices  196 us (60%)
  matrix products  73.1 us (23%)
  blocking collectives  22.9 us (7%)
  between operations  14.3 us (4%)
  starting transfers between devices  11 us (3%)
  local copies, waits for them, and re-layouts  4.61 us (1%)
    psum x1, waiting for transfers between devices, per_device(): total = lax.psum(partial_value, 'col')  148 us
    all_gather x1, waiting for transfers between devices, per_device(): lax.all_gather(normals, 'row', axis=0, tiled=True)  35.4 us
    dot_general x4, matrix products, pair_terms(): jnp.dot(back_first, radial_weight.T, preferred_element_type=jnp.float32)  35 us
    all_gather x1, blocking collectives, per_device(): whole = lax.all_gather(slab, 'row', axis=0, tiled=True)  22.9 us
    dot_general x4, matrix products, pair_terms(): jnp.dot(first.astype(jnp.bfloat16), middle_weight, preferred_element_type...  18.1 us
    ppermute x2, starting transfers between devices, with_halo(): lax.ppermute(tail, axis, [(i, (i + 1) % count) for i in range(count)])  10.3 us
    dot_general x1, matrix products, per_device(): jnp.dot(factor_panel, lax.all_gather(normals, 'row', axis=0, tiled=True),...  10.2 us
    dot_general x4, matrix products, pair_terms(): jnp.dot(flat_basis.astype(jnp.bfloat16), radial_weight, preferred_element...  9.83 us
  transfers between devices with their start and end apart: 6, of which 6 were waited for; matrix products, arithmetic and copies ran while one was open for 0% of the time, Pallas kernels for 0%

commit v1 on v0

--- a/solution.py
+++ b/solution.py
@@ -85,7 +85,8 @@
     col_count = lax.axis_size("col")
     col_index = lax.axis_index("col")
     slab_rows = local_rows // col_count
-    total = lax.psum(partial_value, "col")
+    parts = lax.all_gather(partial_value, "col")
+    total = jnp.sum(parts, axis=0)
     slab = lax.dynamic_slice_in_dim(total, col_index * slab_rows, slab_rows, 0)
     rows_count = lax.axis_size("row")
     row_index = lax.axis_index("row")

time: 324 us -> 277 us (0.85)
  waiting for transfers between devices: 196 us -> 143 us
  other arithmetic: 1.69 us -> 6.96 us
    psum x1 -> x0, waiting for transfers between devices: 148 us -> none  [per_device(): total = lax.psum(partial_value, 'col')]
    all_gather x0 -> x1, waiting for transfers between devices: none -> 95.5 us  [per_device(): parts = lax.all_gather(partial_value, 'col')]
    reduce_sum x0 -> x1, other arithmetic: none -> 5.27 us  [per_device(): total = jnp.sum(parts, axis=0)]
where the time goes in v1:
time: 277 us
  waiting for transfers between devices  143 us (52%)
  matrix products  72.9 us (26%)
  blocking collectives  22.6 us (8%)
  between operations  14.3 us (5%)
  starting transfers between devices  12.6 us (5%)
  other arithmetic  6.96 us (3%)
  local copies, waits for them, and re-layouts  3.82 us (1%)
    all_gather x1, waiting for transfers between devices, per_device(): parts = lax.all_gather(partial_value, 'col')  95.5 us
    all_gather x1, waiting for transfers between devices, per_device(): lax.all_gather(normals, 'row', axis=0, tiled=True)  35.4 us
    dot_general x4, matrix products, pair_terms(): jnp.dot(back_first, radial_weight.T, preferred_element_type=jnp.float32)  34.9 us
    all_gather x1, blocking collectives, per_device(): whole = lax.all_gather(slab, 'row', axis=0, tiled=True)  22.6 us
    dot_general x4, matrix products, pair_terms(): jnp.dot(first.astype(jnp.bfloat16), middle_weight, preferred_element_type...  18.1 us
    ppermute x2, starting transfers between devices, with_halo(): lax.ppermute(tail, axis, [(i, (i + 1) % count) for i in range(count)])  11.8 us
    dot_general x1, matrix products, per_device(): jnp.dot(factor_panel, lax.all_gather(normals, 'row', axis=0, tiled=True),...  10.2 us
    dot_general x4, matrix products, pair_terms(): jnp.dot(flat_basis.astype(jnp.bfloat16), radial_weight, preferred_element...  9.82 us
  transfers between devices with their start and end apart: 6, of which 6 were waited for; matrix products, arithmetic and copies ran while one was open for 0% of the time, Pallas kernels for 0%

profile of v1, /device:TPU:103, one launch (start us, length us, event | category | flops | bytes accessed | tf_op | source)
XLA Modules:
  0.0 277.0 jit_solution(8521612550738920961)
XLA Ops:
  8.0 35.4 %all-gather.4.cloned.1.call-done = bf16[6144,128]{1,0:T(8,128)(2,1)} async-done(((bf16[768,128]{1,0:T(8,128)(2,1)}), bf16[6144,128]{1,0:T(8,128)(2,1)}) %all-gather.4.cloned.1.call-update) | async-done | bytes 1572880 | tf_op jit(solution)/shard_map/all_gather | solution.py:82
  43.4 10.2 %fusion.22 = f32[1536,128]{1,0:T(8,128)} fusion(bf16[1536,6144]{1,0:T(8,128)(2,1)} %param.12, bf16[6144,128]{1,0:T(8,128)(2,1)} %all-gather.4.cloned.1.call-done), kind=kOutput, calls=%fused_computation.54 | convolution fusion | flops 2415919104 | bytes 21233664 | tf_op jit(solution)/shard_map/dot_general | solution.py:80
  53.9 95.5 %all-gather.6.cloned.1.call-done = f32[24576,128]{1,0:T(8,128)} async-done(((f32[1536,128]{1,0:T(8,128)}), f32[24576,128]{1,0:T(8,128)}) %all-gather.6.cloned.1.call-update) | async-done | bytes 12582928 | tf_op jit(solution)/shard_map/all_gather | solution.py:88
  149.4 5.3 %reduce_sum.69 = f32[1536,128]{1,0:T(8,128)S(1)} reduce(f32[16,1536,128]{2,1,0:T(8,128)} %bitcast.88, f32[]{:T(128)} %constant.102.clone.1), dimensions={0}, to_apply=%region_0.0 | reduce | flops 2949120 | bytes 13369348 | tf_op jit(solution)/shard_map/reduce_sum | solution.py:89
  154.7 22.6 %all_gather.15 = f32[768,128]{1,0:T(8,128)S(1)} all-gather(f32[96,128]{1,0:T(8,128)S(1)} %constant_dynamic-slice_fusion.1), channel_id=1, replica_groups=mesh['row'=8,'col'=16] {'row'}, dimensions={0}, use_global_device_ids=true | all-gather | bytes 442368 | tf_op jit(solution)/shard_map/all_gather | solution.py:94
  179.8 1.6 collective-permute-done
  181.4 2.4 collective-permute-done.1
  183.8 11.0 %collective-permute-start.2 = (f32[3,1,3,16,128]{4,2,3,1,0:T(4,128)S(1)}, f32[3,1,3,16,128]{4,2,3,1,0:T(4,128)S(1)}, u32[]{:S(2)}, u32[]{:S(2)}) collective-permute-start(f32[3,1,3,16,128]{4,2,3,1,0:T(4,128)S(1)} %pad_maximum_fusion.2), channel_id=1, source_target_pairs={{0,1},{1,2},{2,3},{3,4},{4,5},{5,6},{6,7},{7,8},{8,9},{9,10},{10,1... | collective-permute-start | bytes 221192 | tf_op jit(solution)/shard_map/ppermute | solution.py:16
  194.8 1.6 collective-permute-done.2
  196.5 6.0 %collective-permute-done.3 = f32[3,1,3,16,128]{4,2,3,1,0:T(4,128)S(1)} collective-permute-done((f32[3,1,3,16,128]{4,2,3,1,0:T(4,128)S(1)}, f32[3,1,3,16,128]{4,2,3,1,0:T(4,128)S(1)}, u32[]{:S(2)}, u32[]{:S(2)}) %collective-permute-start.3) | collective-permute-done | bytes 73760 | tf_op jit(solution)/shard_map/ppermute | solution.py:18
  202.6 2.0 gather_fusion.1
  204.9 64.6 %while.14 = (s32[]{:T(128)}, f32[4,8,128]{2,1,0:T(8,128)S(1)}, f32[4,3,8,128]{3,2,1,0:T(8,128)S(1)}, f32[4,3,8,12]{3,2,0,1:T(8,128)S(1)}, f32[4,3,8,12,128]{4,3,...) while((s32[]{:T(128)}, f32[4,8,128]{2,1,0:T(8,128)S(1)}, ...), condition=%wide.region_7.8_spmd, body=%wide.region_1.7_spmd.sunk | while | flops 1651777664 | bytes 57794740 | solution.py:117
  205.1 2.5 fusion.42
  207.6 4.5 %multiply_reduce_fusion.7 = (f32[12288]{0:T(1024)S(1)}, f32[12288,128]{1,0:T(8,128)}) fusion(f32[128]{0:T(128)S(1)} %get-tuple-element.295, f32[128]{0:T(128)S(1)} %get-tuple-element.294, bf16[128,128]{1,0:T(8,128)(2,1)S(1)} %get-tuple-element.293, f32[12288,128]{1,0:T(8,128)S(1)} %fusion.42), kind=kOutput, calls=%fused_computation.15.clone.1 | convolution fusion | flops 408932352 | bytes 12665856 | tf_op jit(solution)/shard_map/while/body/eval_jaxpr/dot_general | solution.py:49
  212.1 8.7 %fusion.43 = f32[12288]{0:T(1024)S(1)} fusion(f32[128]{0:T(128)S(1)} %iota_multiply_fusion.2, f32[12288]{0:T(1024)S(1)} %sub.114, bf16[128,128]{1,0:T(8,128)(2,1)S(1)} %get-tuple-element.291, bf16[128,128]{1,0:T(8,128)(2,1)S(1)} %get-tuple-element.293, f32[12288,128]{1,0:T(8,128)} %copy-done, f32[12288,128]{1,0:T(8,128)} %get-tuple-element.258, ...), kind=kOutput, calls=%fused_computation.23.clone.1 | convolution fusion | flops 830459904 | bytes 12747776 | tf_op jit(solution)/shard_map/while/body/eval_jaxpr/dot_general | solution.py:58
  221.2 2.5 fusion.42
  223.7 4.5 %multiply_reduce_fusion.7 = (f32[12288]{0:T(1024)S(1)}, f32[12288,128]{1,0:T(8,128)}) fusion(f32[128]{0:T(128)S(1)} %get-tuple-element.295, f32[128]{0:T(128)S(1)} %get-tuple-element.294, bf16[128,128]{1,0:T(8,128)(2,1)S(1)} %get-tuple-element.293, f32[12288,128]{1,0:T(8,128)S(1)} %fusion.42), kind=kOutput, calls=%fused_computation.15.clone.1 | convolution fusion | flops 408932352 | bytes 12665856 | tf_op jit(solution)/shard_map/while/body/eval_jaxpr/dot_general | solution.py:49
  228.2 8.7 %fusion.43 = f32[12288]{0:T(1024)S(1)} fusion(f32[128]{0:T(128)S(1)} %iota_multiply_fusion.2, f32[12288]{0:T(1024)S(1)} %sub.114, bf16[128,128]{1,0:T(8,128)(2,1)S(1)} %get-tuple-element.291, bf16[128,128]{1,0:T(8,128)(2,1)S(1)} %get-tuple-element.293, f32[12288,128]{1,0:T(8,128)} %copy-done, f32[12288,128]{1,0:T(8,128)} %get-tuple-element.258, ...), kind=kOutput, calls=%fused_computation.23.clone.1 | convolution fusion | flops 830459904 | bytes 12747776 | tf_op jit(solution)/shard_map/while/body/eval_jaxpr/dot_general | solution.py:58
  237.4 2.5 fusion.42
  239.9 4.5 %multiply_reduce_fusion.7 = (f32[12288]{0:T(1024)S(1)}, f32[12288,128]{1,0:T(8,128)}) fusion(f32[128]{0:T(128)S(1)} %get-tuple-element.295, f32[128]{0:T(128)S(1)} %get-tuple-element.294, bf16[128,128]{1,0:T(8,128)(2,1)S(1)} %get-tuple-element.293, f32[12288,128]{1,0:T(8,128)S(1)} %fusion.42), kind=kOutput, calls=%fused_computation.15.clone.1 | convolution fusion | flops 408932352 | bytes 12665856 | tf_op jit(solution)/shard_map/while/body/eval_jaxpr/dot_general | solution.py:49
  244.4 8.7 %fusion.43 = f32[12288]{0:T(1024)S(1)} fusion(f32[128]{0:T(128)S(1)} %iota_multiply_fusion.2, f32[12288]{0:T(1024)S(1)} %sub.114, bf16[128,128]{1,0:T(8,128)(2,1)S(1)} %get-tuple-element.291, bf16[128,128]{1,0:T(8,128)(2,1)S(1)} %get-tuple-element.293, f32[12288,128]{1,0:T(8,128)} %copy-done, f32[12288,128]{1,0:T(8,128)} %get-tuple-element.258, ...), kind=kOutput, calls=%fused_computation.23.clone.1 | convolution fusion | flops 830459904 | bytes 12747776 | tf_op jit(solution)/shard_map/while/body/eval_jaxpr/dot_general | solution.py:58
  253.5 2.5 fusion.42
  256.0 4.5 %multiply_reduce_fusion.7 = (f32[12288]{0:T(1024)S(1)}, f32[12288,128]{1,0:T(8,128)}) fusion(f32[128]{0:T(128)S(1)} %get-tuple-element.295, f32[128]{0:T(128)S(1)} %get-tuple-element.294, bf16[128,128]{1,0:T(8,128)(2,1)S(1)} %get-tuple-element.293, f32[12288,128]{1,0:T(8,128)S(1)} %fusion.42), kind=kOutput, calls=%fused_computation.15.clone.1 | convolution fusion | flops 408932352 | bytes 12665856 | tf_op jit(solution)/shard_map/while/body/eval_jaxpr/dot_general | solution.py:49
  260.5 8.7 %fusion.43 = f32[12288]{0:T(1024)S(1)} fusion(f32[128]{0:T(128)S(1)} %iota_multiply_fusion.2, f32[12288]{0:T(1024)S(1)} %sub.114, bf16[128,128]{1,0:T(8,128)(2,1)S(1)} %get-tuple-element.291, bf16[128,128]{1,0:T(8,128)(2,1)S(1)} %get-tuple-element.293, f32[12288,128]{1,0:T(8,128)} %copy-done, f32[12288,128]{1,0:T(8,128)} %get-tuple-element.258, ...), kind=kOutput, calls=%fused_computation.23.clone.1 | convolution fusion | flops 830459904 | bytes 12747776 | tf_op jit(solution)/shard_map/while/body/eval_jaxpr/dot_general | solution.py:58
  (99 shorter events, 5.8 us)
Async XLA Ops:
  7.2 36.2 %all-gather.4.cloned.1.call-start = ((), (), s32[]{:S(2)}) async-start(), calls=%async_computation | async-start | bytes 1769472 | tf_op jit(solution)/shard_map/all_gather | solution.py:82
  7.9 45.7 %copy-start.5 = (s32[32,12]{0,1:T(8,128)S(1)}, s32[32,12]{0,1:T(8,128)}, u32[]{:S(2)}) copy-start(s32[32,12]{0,1:T(8,128)} %param.15) | copy-start | bytes 4612
  7.9 45.9 %copy-start.8 = (s32[1,16]{1,0:T(1,128)S(1)}, s32[1,16]{1,0:T(1,128)}, u32[]{:S(2)}) copy-start(s32[1,16]{1,0:T(1,128)} %param.16) | copy-start | bytes 196
  7.9 141.4 %all-gather.6.cloned.1.call-start = ((), (), s32[]{:S(2)}) async-start(), calls=%async_computation.1 | async-start | bytes 13369344 | tf_op jit(solution)/shard_map/all_gather | solution.py:88
  149.4 30.3 %copy-start.2 = (f32[3,32,12]{1,2,0:T(8,128)S(1)}, f32[3,32,12]{1,2,0:T(8,128)}, u32[]{:S(2)}) copy-start(f32[3,32,12]{1,2,0:T(8,128)} %param.14) | copy-start | bytes 13828
  149.4 55.5 %copy-start.1 = (bf16[128,128]{1,0:T(8,128)(2,1)S(1)}, bf16[128,128]{1,0:T(8,128)(2,1)}, u32[]{:S(2)}) copy-start(bf16[128,128]{1,0:T(8,128)(2,1)} %param.19) | copy-start | bytes 98308
  149.4 55.5 %copy-start.3 = (f32[128]{0:T(128)S(1)}, f32[128]{0:T(128)}, u32[]{:S(2)}) copy-start(f32[128]{0:T(128)} %param.20) | copy-start | bytes 1540
  149.4 55.5 %copy-start.4 = (f32[128]{0:T(128)S(1)}, f32[128]{0:T(128)}, u32[]{:S(2)}) copy-start(f32[128]{0:T(128)} %param.21) | copy-start | bytes 1540
  149.4 55.5 %copy-start.6 = (bf16[128,128]{1,0:T(8,128)(2,1)S(1)}, bf16[128,128]{1,0:T(8,128)(2,1)}, u32[]{:S(2)}) copy-start(bf16[128,128]{1,0:T(8,128)(2,1)} %param.17) | copy-start | bytes 98308
  149.4 55.5 %copy-start.9 = (f32[128]{0:T(128)S(1)}, f32[128]{0:T(128)}, u32[]{:S(2)}) copy-start(f32[128]{0:T(128)} %param.18) | copy-start | bytes 1540
  178.1 3.3 %collective-permute-start = (f32[1,1,3,16,128]{4,2,3,1,0:T(4,128)S(1)}, f32[1,1,3,16,128]{4,2,3,1,0:T(4,128)S(1)}, u32[]{:S(2)}, u32[]{:S(2)}) collective-permute-start(f32[1,1,3,16,128]{4,2,3,1,0:T(4,128)S(1)} %bitcast_select_fusion), channel_id=1, source_target_pairs={{0,16},{16,32},{32,48},{48,64},{64,80},{80,96},{96,112},{112,0},{1... | collective-permute-start | bytes 73736 | tf_op jit(solution)/shard_map/ppermute | solution.py:16
  178.9 4.9 %collective-permute-start.1 = (f32[1,1,3,16,128]{4,2,3,1,0:T(4,128)S(1)}, f32[1,1,3,16,128]{4,2,3,1,0:T(4,128)S(1)}, u32[]{:S(2)}, u32[]{:S(2)}) collective-permute-start(f32[1,1,3,16,128]{4,2,3,1,0:T(4,128)S(1)} %bitcast_select_fusion), channel_id=1, source_target_pairs={{16,0},{32,16},{48,32},{64,48},{80,64},{96,80},{112,96},{0,112},{1... | collective-permute-start | bytes 73736 | tf_op jit(solution)/shard_map/ppermute | solution.py:18
  183.8 12.7 %collective-permute-start.2 = (f32[3,1,3,16,128]{4,2,3,1,0:T(4,128)S(1)}, f32[3,1,3,16,128]{4,2,3,1,0:T(4,128)S(1)}, u32[]{:S(2)}, u32[]{:S(2)}) collective-permute-start(f32[3,1,3,16,128]{4,2,3,1,0:T(4,128)S(1)} %pad_maximum_fusion.2), channel_id=1, source_target_pairs={{0,1},{1,2},{2,3},{3,4},{4,5},{5,6},{6,7},{7,8},{8,9},{9,10},{10,1... | collective-permute-start | bytes 221192 | tf_op jit(solution)/shard_map/ppermute | solution.py:16
  194.8 7.7 %collective-permute-start.3 = (f32[3,1,3,16,128]{4,2,3,1,0:T(4,128)S(1)}, f32[3,1,3,16,128]{4,2,3,1,0:T(4,128)S(1)}, u32[]{:S(2)}, u32[]{:S(2)}) collective-permute-start(f32[3,1,3,16,128]{4,2,3,1,0:T(4,128)S(1)} %pad_maximum_fusion.2), channel_id=1, source_target_pairs={{1,0},{2,1},{3,2},{4,3},{5,4},{6,5},{7,6},{8,7},{9,8},{10,9},{11,1... | collective-permute-start | bytes 221192 | tf_op jit(solution)/shard_map/ppermute | solution.py:18
  207.6 4.5 %copy-start = (f32[12288,128]{1,0:T(8,128)}, f32[12288,128]{1,0:T(8,128)S(1)}, u32[]{:S(2)}) copy-start(f32[12288,128]{1,0:T(8,128)S(1)} %fusion.42) | copy-start | bytes 18874372 | tf_op jit(solution)/shard_map/while
  223.7 4.5 %copy-start = (f32[12288,128]{1,0:T(8,128)}, f32[12288,128]{1,0:T(8,128)S(1)}, u32[]{:S(2)}) copy-start(f32[12288,128]{1,0:T(8,128)S(1)} %fusion.42) | copy-start | bytes 18874372 | tf_op jit(solution)/shard_map/while
  239.9 4.5 %copy-start = (f32[12288,128]{1,0:T(8,128)}, f32[12288,128]{1,0:T(8,128)S(1)}, u32[]{:S(2)}) copy-start(f32[12288,128]{1,0:T(8,128)S(1)} %fusion.42) | copy-start | bytes 18874372 | tf_op jit(solution)/shard_map/while
  256.0 4.5 %copy-start = (f32[12288,128]{1,0:T(8,128)}, f32[12288,128]{1,0:T(8,128)S(1)}, u32[]{:S(2)}) copy-start(f32[12288,128]{1,0:T(8,128)S(1)} %fusion.42) | copy-start | bytes 18874372 | tf_op jit(solution)/shard_map/while
  269.5 0.6 copy-start.7
Sparse Core Ops, SparseCore 0:
  9.6 33.7 all-gather.3
  53.7 95.5 all-gather.5
